TPU v7x, 256 devices: a whole 4x4x8 slice. The times are simulated.
256 devices in a mesh: dp: 2 (over y_lo), ctx: 16 (over y_hi, z), tensor: 8 (over x, core).
Axes of the slice: x: 4, y: 4 (y_hi: 2, y_lo: 2; y = y_hi * 2 + y_lo), z: 8, core: 2. Of those that a mesh axis runs over, the one named last changes fastest.
Arguments:
- input_spikes: int32 [512, 8192], P(None, ('dp', 'ctx')), may hold values from 0 to 65535
- query_spikes: int32 [512, 8192], P('tensor', ('dp', 'ctx')), may hold values from 0 to 65535
- key_spikes: int32 [512, 8192], P('tensor', ('dp', 'ctx')), may hold values from 0 to 65535
- values: bfloat16 [8192, 8192], P(('dp', 'ctx'), 'tensor'), may hold values from -6 to 6
- query_slope: bfloat16 [8192, 8192], P(('dp', 'ctx'), 'tensor'), may hold values from 0.25 to 2
- key_slope: bfloat16 [8192, 8192], P(('dp', 'ctx'), 'tensor'), may hold values from 0.25 to 2
- grad_out: bfloat16 [8192, 8192], P(('dp', 'ctx'), 'tensor'), may hold values from -6 to 6
- log_gate: float32 [64, 8192], P('tensor', ('dp', 'ctx')), may hold values from -0.8 to 0
- pattern: int32 [128, 16], P('tensor'), may hold values from 0 to 127, all different within a row
Outputs:
- query_grad: bfloat16 [8192, 8192], P(('dp', 'ctx'), 'tensor')
- key_grad: bfloat16 [8192, 8192], P(('dp', 'ctx'), 'tensor')
- value_grad: float32 [16, 128, 4096], P('ctx', 'tensor')
Inputs may be any that keep to these rules, and one draw needn't show every extreme that they name: `pattern`: each column block names 16 different row blocks.
All inputs are finite; a program needn't handle non-finite values.
Results may differ from a plain program's by a relative error of at most 0.0073.
Values sent between devices are 32-bit elements; how exact they have to be, the bound alone decides.
A program may use at most 128 MiB of HBM per device.

v0:
```python
import jax
import jax.numpy as jnp
from jax import lax
from jax.sharding import PartitionSpec as P

D = 8192
HEAD = 128
BLK = 64
SEL = 16
highest = lax.Precision.HIGHEST


def entering(value, axis, combine, identity, reverse):
    devices, place = (lax.axis_size(axis), lax.axis_index(axis))
    everything = jax.tree.map(lambda part: lax.all_gather(part, axis), value)
    start = jax.tree.map(
        lambda part, zero: jnp.broadcast_to(jnp.asarray(zero, part.dtype), part.shape),
        value,
        identity,
    )

    def turn(k, before):
        at = devices - 1 - k if reverse else k
        reached = at > place if reverse else at < place
        new = combine(before, jax.tree.map(lambda part: part[at], everything))
        return jax.tree.map(lambda a, b: jnp.where(reached, a, b), new, before)

    return lax.fori_loop(0, devices, turn, start)


def dims_of(left_dim, right_dim):
    return (((left_dim,), (right_dim,)), ((), ()))


def unpack_flags(packed):
    shifts = jnp.arange(16, dtype=jnp.int32)
    flags = jnp.bitwise_and(jnp.right_shift(packed[:, None, :], shifts[None, :, None]), 1)
    return flags.reshape(packed.shape[0] * 16, packed.shape[1]).astype(jnp.bfloat16)


def decay_matrix(cumulative):
    spread = cumulative[:, None] - cumulative[None, :]
    places = jnp.arange(cumulative.shape[0])
    causal = places[:, None] >= places[None, :]
    return jnp.where(causal, jnp.exp(jnp.minimum(spread, 0.0)), 0.0)


def first_phase(query_cols, key_cols, head_values, cumulative):
    decays = decay_matrix(cumulative)
    intersection = lax.dot_general(
        query_cols, key_cols, dims_of(0, 0), preferred_element_type=jnp.float32
    )
    weights = intersection * decays
    weights_low = weights.astype(jnp.bfloat16)
    local_num = jnp.dot(weights_low, head_values, preferred_element_type=jnp.float32)
    local_den = jnp.sum(weights, axis=1)
    tail_decay = jnp.exp(cumulative[-1] - cumulative)
    key_float = key_cols.astype(jnp.float32) * tail_decay[None, :]
    state_sum = jnp.dot(key_float, head_values.astype(jnp.float32), precision=highest)
    key_sum = jnp.sum(key_float, axis=1)
    return (weights_low, local_num, local_den, jnp.exp(cumulative[-1]), state_sum, key_sum)


def second_phase(
    query_cols,
    key_cols,
    head_values,
    head_grad,
    cumulative,
    weights_low,
    local_num,
    local_den,
    state_in,
    keys_in,
):
    decays = decay_matrix(cumulative)
    lead_decay = jnp.exp(cumulative)
    query_float = query_cols.astype(jnp.float32)
    carried_num = lax.dot_general(query_float, state_in, dims_of(0, 0), precision=highest)
    numerator = local_num + lead_decay[:, None] * carried_num
    denominator = 1.0 + local_den + lead_decay * jnp.dot(keys_in, query_float, precision=highest)
    output = numerator / denominator[:, None]
    grad_float = head_grad.astype(jnp.float32)
    scaled = grad_float / denominator[:, None]
    norm_grad = -jnp.sum(grad_float * output, axis=1) / denominator
    scaled_low = scaled.astype(jnp.bfloat16)
    cross_term = lax.dot_general(
        scaled_low, head_values, dims_of(1, 1), preferred_element_type=jnp.float32
    )
    mixed_low = ((cross_term + norm_grad[:, None]) * decays).astype(jnp.bfloat16)
    carried_query = (
        lax.dot_general(scaled, state_in, dims_of(1, 1), precision=highest)
        + norm_grad[:, None] * keys_in[None, :]
    )
    grad_query = (
        lax.dot_general(mixed_low, key_cols, dims_of(1, 1), preferred_element_type=jnp.float32)
        + lead_decay[:, None] * carried_query
    )
    grad_key = lax.dot_general(
        mixed_low, query_cols, dims_of(0, 1), preferred_element_type=jnp.float32
    )
    grad_value = lax.dot_general(
        weights_low, scaled_low, dims_of(0, 0), preferred_element_type=jnp.float32
    )
    adjoint_sum = jnp.dot(query_float * lead_decay[None, :], scaled, precision=highest)
    adjoint_vec = jnp.dot(query_float, lead_decay * norm_grad, precision=highest)
    return (grad_query, grad_key, grad_value, adjoint_sum, adjoint_vec)


def third_phase(
    key_cols, head_values, cumulative, grad_key_local, grad_value_local, adjoint, adjoint_vec
):
    tail_decay = jnp.exp(cumulative[-1] - cumulative)[:, None]
    value_float = head_values.astype(jnp.float32)
    key_float = key_cols.astype(jnp.float32)
    grad_key = grad_key_local + tail_decay * (
        lax.dot_general(value_float, adjoint, dims_of(1, 1), precision=highest)
        + adjoint_vec[None, :]
    )
    grad_value = grad_value_local + tail_decay * lax.dot_general(
        key_float, adjoint, dims_of(0, 0), precision=highest
    )
    return (grad_key, grad_value)


def combine_forward(earlier_part, later_part):
    total_early, state_early, keys_early = earlier_part
    total_late, state_late, keys_late = later_part
    return (
        total_early * total_late,
        total_late[:, None, None] * state_early + state_late,
        total_late[:, None] * keys_early + keys_late,
    )


def combine_backward(earlier_part, later_part):
    total_early, adjoint_early, vector_early = earlier_part
    total_late, adjoint_late, vector_late = later_part
    return (
        total_early * total_late,
        adjoint_late + total_late[:, None, None] * adjoint_early,
        vector_late + total_late[:, None] * vector_early,
    )


def run_first(block_items):
    return first_phase(*block_items)


def run_second(block_items):
    return second_phase(*block_items)


def per_device(
    input_spikes,
    query_spikes,
    key_spikes,
    values,
    query_slope,
    key_slope,
    grad_out,
    log_gate,
    pattern,
):
    tokens_here = values.shape[0]
    heads_here = values.shape[1] // HEAD
    query_cols = unpack_flags(query_spikes).reshape(heads_here, HEAD, tokens_here)
    key_cols = unpack_flags(key_spikes).reshape(heads_here, HEAD, tokens_here)
    head_values = values.reshape(tokens_here, heads_here, HEAD).transpose(1, 0, 2)
    head_grads = grad_out.reshape(tokens_here, heads_here, HEAD).transpose(1, 0, 2)
    cumulative = jnp.cumsum(log_gate, axis=1)
    weights_low, local_num, local_den, totals, state_sum, key_sum = lax.map(
        run_first, (query_cols, key_cols, head_values, cumulative)
    )
    identity_state = (
        jnp.ones((heads_here,), jnp.float32),
        jnp.zeros((heads_here, HEAD, HEAD), jnp.float32),
        jnp.zeros((heads_here, HEAD), jnp.float32),
    )
    carried_state = entering(
        (totals, state_sum, key_sum), "ctx", combine_forward, identity_state, False
    )
    grad_query, grad_key_local, grad_value_local, adjoint_sum, adjoint_vec = lax.map(
        run_second,
        (
            query_cols,
            key_cols,
            head_values,
            head_grads,
            cumulative,
            weights_low,
            local_num,
            local_den,
            carried_state[1],
            carried_state[2],
        ),
    )
    carried_adjoint = entering(
        (totals, adjoint_sum, adjoint_vec), "ctx", combine_backward, identity_state, True
    )
    grad_key, grad_value = jax.vmap(third_phase)(
        key_cols,
        head_values,
        cumulative,
        grad_key_local,
        grad_value_local,
        carried_adjoint[1],
        carried_adjoint[2],
    )
    width_here = heads_here * HEAD
    flat_query = grad_query.transpose(1, 0, 2).reshape(tokens_here, width_here)
    flat_key = grad_key.transpose(1, 0, 2).reshape(tokens_here, width_here)
    query_grad = (query_slope.astype(jnp.float32) * flat_query).astype(jnp.bfloat16)
    key_grad = (key_slope.astype(jnp.float32) * flat_key).astype(jnp.bfloat16)
    column_blocks = pattern.shape[0]
    value_low = grad_value.transpose(1, 0, 2).reshape(tokens_here, width_here).astype(jnp.bfloat16)
    value_blocks = value_low.reshape(tokens_here, column_blocks, BLK)
    input_cols = unpack_flags(input_spikes)
    row_share = SEL // lax.axis_size("ctx")
    input_blocks = input_cols.reshape(D // BLK, BLK, tokens_here)
    chosen = pattern.T
    gathered = jnp.take(input_blocks, chosen, axis=0)
    partial_value = jnp.einsum(
        "snat,tnb->snab", gathered, value_blocks, preferred_element_type=jnp.float32
    )
    reduced = lax.psum_scatter(
        partial_value.reshape(lax.axis_size("ctx") * row_share, column_blocks, BLK * BLK),
        "ctx",
        scatter_dimension=0,
        tiled=True,
    )
    value_grad = lax.psum(reduced, "dp")
    return (query_grad, key_grad, value_grad)


def solution(mesh):
    in_specs = (
        P(None, ("dp", "ctx")),
        P("tensor", ("dp", "ctx")),
        P("tensor", ("dp", "ctx")),
        P(("dp", "ctx"), "tensor"),
        P(("dp", "ctx"), "tensor"),
        P(("dp", "ctx"), "tensor"),
        P(("dp", "ctx"), "tensor"),
        P("tensor", ("dp", "ctx")),
        P("tensor", None),
    )
    out_specs = (P(("dp", "ctx"), "tensor"), P(("dp", "ctx"), "tensor"), P("ctx", "tensor", None))
    return jax.shard_map(
        per_device, mesh=mesh, in_specs=in_specs, out_specs=out_specs, check_vma=False
    )
```

profile of v0, /device:TPU:1, one launch (start us, length us, event | category | flops | bytes accessed | tf_op | source)
XLA Modules:
  0.0 712.7 jit_solution(3989834290211773359)
XLA Ops:
  7.3 1.2 reduce-window.6
  8.9 1.2 copy.49
  12.6 34.4 %while.72 = (s32[]{:T(128)}, bf16[8,256,256]{1,2,0:T(8,128)(2,1)}, f32[8,256,128]{2,1,0:T(8,128)}, f32[8,256]{1,0:T(8,128)S(1)}, f32[8]{0:T(128)S(1)}, /*index=5...) while((s32[]{:T(128)}, bf16[8,256,256]{1,2,0:T(8,128)(2,1)}, ...), condition=%wide.region_5.6_spmd, body=%wide.region_2.5_spmd.sunk | while | flops 84574080 | bytes 1523417 | solution.py:172
  48.0 2.0 copy.48
  51.6 39.0 %all-reduce = f32[128]{0:T(128)S(1)} all-reduce(f32[128]{0:T(128)S(1)} %dynamic-update-slice), channel_id=2, replica_groups=mesh['dp'=2,'ctx'=16,'tensor'=8] {'ctx'}, use_global_device_ids=true, to_apply=%add | all-reduce | flops 128 | bytes 1024
  90.6 29.6 %all-gather.2 = f32[128,128]{1,0:T(8,128)S(1)} all-gather(f32[8,128]{1,0:T(8,128)S(1)} %get-tuple-element.456), channel_id=4, replica_groups=mesh['dp'=2,'ctx'=16,'tensor'=8] {'ctx'}, dimensions={0}, use_global_device_ids=true | all-gather | bytes 69632 | tf_op jit(solution)/shard_map/all_gather | solution.py:15
  120.2 66.5 %all-gather.8.cloned.1.call-done = f32[128,128,128]{2,1,0:T(8,128)} async-done(((f32[8,128,128]{2,1,0:T(8,128)}), f32[128,128,128]{2,1,0:T(8,128)}) %all-gather.8.cloned.1.call-update) | async-done | bytes 8388624 | tf_op jit(solution)/shard_map/all_gather | solution.py:15
  186.7 20.1 %while.74 = (s32[]{:T(128)}, f32[8,128,128]{2,1,0:T(8,128)S(1)}, f32[8,128]{1,0:T(8,128)S(1)}, s32[]{:T(128)}, f32[16,8]{1,0:T(8,128)S(1)}, /*index=5*/f32[16,8,...) while((s32[]{:T(128)}, f32[8,128,128]{2,1,0:T(8,128)S(1)}, ...), condition=%wide.region_7.8_spmd.clone, body=%wide.region_6.7_spmd.clone.sunk | while | flops 528388 | bytes 1585415 | solution.py:28
  187.9 1.2 fusion.185
  189.2 1.2 fusion.185
  190.4 1.2 fusion.185
  191.7 1.2 fusion.185
  193.0 1.2 fusion.185
  194.2 1.2 fusion.185
  195.5 1.2 fusion.185
  196.7 1.2 fusion.185
  198.0 1.2 fusion.185
  199.2 1.2 fusion.185
  205.5 1.2 fusion.185
  206.8 75.2 %while.73 = (s32[]{:T(128)}, f32[8,256,128]{1,2,0:T(8,128)}, f32[8,256,128]{1,2,0:T(8,128)}, f32[8,256,128]{1,2,0:T(8,128)}, f32[8,128,128]{2,1,0:T(8,128)S(1)},...) while((s32[]{:T(128)}, f32[8,256,128]{1,2,0:T(8,128)}, ...), condition=%wide.region_10.11_spmd, body=%wide.region_8.10_spmd.sunk | while | flops 220071168 | bytes 2862273 | solution.py:183
  213.1 1.8 fusion.181
  222.5 1.8 fusion.181
  231.9 1.8 fusion.181
  241.3 1.8 fusion.181
  250.7 1.8 fusion.181
  260.1 1.8 fusion.181
  269.5 1.8 fusion.181
  278.9 1.8 fusion.181
  283.3 1.7 shift_right_arithmetic.72
  285.0 3.7 fusion.81
  288.7 10.9 %gather_fusion = bf16[256,64,256]{2,1,0:T(8,128)(2,1)} fusion(bf16[128,64,256]{2,1,0:T(8,128)(2,1)} %fusion.81, s32[1024]{0:T(1024)S(1)} %pad_clamp_fusion), kind=kCustom, calls=%fused_computation | custom fusion | bytes 16778240 | tf_op jit(solution)/shard_map/jit(_take)/gather | solution.py:222
  299.9 30.1 %all-gather.4 = f32[128,128]{1,0:T(8,128)S(1)} all-gather(f32[8,128]{1,0:T(8,128)S(1)} %get-tuple-element.464), channel_id=6, replica_groups=mesh['dp'=2,'ctx'=16,'tensor'=8] {'ctx'}, dimensions={0}, use_global_device_ids=true | all-gather | bytes 69632 | tf_op jit(solution)/shard_map/all_gather | solution.py:15
  330.0 84.7 %all-gather.10.cloned.1.call-done = f32[128,128,128]{2,1,0:T(8,128)} async-done(((f32[8,128,128]{2,1,0:T(8,128)}), f32[128,128,128]{2,1,0:T(8,128)}) %all-gather.10.cloned.1.call-update) | async-done | bytes 8388624 | tf_op jit(solution)/shard_map/all_gather | solution.py:15
  414.7 20.1 %while.75 = (s32[]{:T(128)}, f32[8,128,128]{2,1,0:T(8,128)S(1)}, f32[8,128]{1,0:T(8,128)S(1)}, s32[]{:T(128)}, f32[16,8,128,128]{3,2,1,0:T(8,128)}, /*index=5*/f...) while((s32[]{:T(128)}, f32[8,128,128]{2,1,0:T(8,128)S(1)}, ...), condition=%wide.region_12.13_spmd.clone, body=%wide.region_11.12_spmd.clone.sunk | while | flops 528392 | bytes 1585477 | solution.py:28
  416.0 1.2 fusion.188
  422.3 1.2 fusion.188
  423.5 1.2 fusion.188
  429.8 1.2 fusion.188
  431.1 1.2 fusion.188
  435.5 8.6 %fusion.84 = f32[16,16,64,64]{2,3,0,1:T(8,128)} fusion(bf16[256,16,64,1]{0,2,3,1:T(8,128)(2,1)S(1)} %bitcast.307, bf16[16,16,64,256]{3,2,1,0:T(8,128)(2,1)} %bitcast.298, pred[16,16]{1,0:T(8,128)(4,1)S(1)} %copy.63), kind=kOutput, calls=%fused_computation.118 | convolution fusion | flops 541065216 | bytes 13107456 | tf_op jit(solution)/shard_map/snat,tnb->snab/dot_general | solution.py:223
  444.1 9.3 %copy.66 = f32[16,16,64,64]{3,2,1,0:T(8,128)} copy(f32[16,16,64,64]{2,3,0,1:T(8,128)} %fusion.84) | data formatting | bytes 8388608 | tf_op jit(solution)/shard_map/snat,tnb->snab/transpose | solution.py:223
  453.3 8.0 %reshape.163 = f32[16,16,4096]{2,1,0:T(8,128)} reshape(f32[16,16,64,64]{3,2,1,0:T(8,128)} %copy.66) | data formatting | bytes 8388608 | tf_op jit(solution)/shard_map/reshape | solution.py:227
  461.4 1.3 copy.72
  462.7 1.9 fusion.90
  464.9 200.6 %reduce-scatter.2.cloned.1.call-done = f32[1,16,4096]{2,1,0:T(8,128)} async-done(((f32[16,16,4096]{2,1,0:T(8,128)}), f32[1,16,4096]{2,1,0:T(8,128)}) %reduce-scatter.2.cloned.1.call-update) | async-done | bytes 262160 | tf_op jit(solution)/shard_map/reduce_scatter | solution.py:226
  665.5 2.7 multiply_convert_fusion
  668.2 36.3 %all-reduce.3.cloned.1.call-done = f32[1,16,4096]{2,1,0:T(8,128)} async-done(((f32[1,16,4096]{2,1,0:T(8,128)}), f32[1,16,4096]{2,1,0:T(8,128)}) %all-reduce.3.cloned.1.call-update) | async-done | bytes 262160 | tf_op jit(solution)/shard_map/psum | solution.py:232
  704.5 1.7 copy.160
  (343 shorter events, 117.5 us)
Async XLA Ops:
  7.2 179.5 %all-gather.8.cloned.1.call-start = ((), (), s32[]{:S(2)}) async-start(), calls=%async_computation.3 | async-start | bytes 8912896 | tf_op jit(solution)/shard_map/all_gather | solution.py:15
  10.1 39.9 %copy-start.6 = (u32[256]{0:T(256)S(1)}, u32[256]{0:T(256)}, u32[]{:S(2)}) copy-start(u32[256]{0:T(256)} %constant.157) | copy-start | bytes 3076
  47.0 0.8 copy-start
  47.9 366.9 %all-gather.10.cloned.1.call-start = ((), (), s32[]{:S(2)}) async-start(), calls=%async_computation.4 | async-start | bytes 8912896 | tf_op jit(solution)/shard_map/all_gather | solution.py:15
  206.8 76.2 %copy-start.5 = (s32[16,16]{1,0:T(8,128)S(1)}, s32[16,16]{1,0:T(8,128)}, u32[]{:S(2)}) copy-start(s32[16,16]{1,0:T(8,128)} %param.25) | copy-start | bytes 3076
  282.0 0.8 copy-start.1
  282.8 382.7 %reduce-scatter.2.cloned.1.call-start = ((), (), s32[]{:S(2)}) async-start(), calls=%async_computation.1 | async-start | bytes 4456448 | tf_op jit(solution)/shard_map/reduce_scatter | solution.py:226
  288.7 146.1 %copy-start.3 = (f32[8,256,128]{1,2,0:T(8,128)S(1)}, f32[8,256,128]{1,2,0:T(8,128)}, u32[]{:S(2)}) copy-start(f32[8,256,128]{1,2,0:T(8,128)} %get-tuple-element.467) | copy-start | bytes 3145732
  453.3 8.1 %copy-start.2 = (f32[8,256,128]{1,2,0:T(8,128)S(1)}, f32[8,256,128]{1,2,0:T(8,128)}, u32[]{:S(2)}) copy-start(f32[8,256,128]{1,2,0:T(8,128)} %get-tuple-element.461) | copy-start | bytes 3145732
  461.3 204.2 %copy-start.4 = (bf16[256,1024]{1,0:T(8,128)(2,1)S(1)}, bf16[256,1024]{1,0:T(8,128)(2,1)}, u32[]{:S(2)}) copy-start(bf16[256,1024]{1,0:T(8,128)(2,1)} %param.22) | copy-start | bytes 1572868
  461.4 243.2 %all-reduce.3.cloned.1.call-start = ((), (), s32[]{:S(2)}) async-start(), calls=%async_computation.2 | async-start | bytes 524288 | tf_op jit(solution)/shard_map/psum | solution.py:232
Sparse Core Ops, SparseCore 0:
  48.0 138.6 all-gather.7
  282.9 131.7 all-gather.9
  461.5 203.9 reduce-scatter.1
  667.9 36.5 all-reduce.2
where the time goes:
time: 717 us; the launch traced here: 713 us
  waiting for transfers between devices  388 us (54%)
  blocking collectives  98.6 us (14%)
  matrix products  92.2 us (13%)
  local copies, waits for them, and re-layouts  57.3 us (8%)
  other arithmetic  54.8 us (8%)
  between operations  14.8 us (2%)
    reduce_scatter x1, waiting for transfers between devices, per_device(): lax.psum_scatter(partial_value.reshape(lax.axis_size('ctx') * row_share,...  201 us
    all_gather x2, waiting for transfers between devices, entering(): everything = jax.tree.map(lambda part: lax.all_gather(part, axis), value)  151 us
    all_gather x2, blocking collectives, entering(): everything = jax.tree.map(lambda part: lax.all_gather(part, axis), value)  59.7 us
    select_n x64, other arithmetic, turn(): return jax.tree.map(lambda a, b: jnp.where(reached, a, b), new, before)  39.8 us
    unnamed x1, blocking collectives  39 us
    psum x1, waiting for transfers between devices, per_device(): value_grad = lax.psum(reduced, 'dp')  36.3 us
  transfers between devices with their start and end apart: 4, of which 4 were waited for; matrix products, arithmetic and copies ran while one was open for 4% of the time, Pallas kernels for 0%

commit v1 on v0

--- a/solution.py
+++ b/solution.py
@@ -229,7 +229,7 @@
         scatter_dimension=0,
         tiled=True,
     )
-    value_grad = lax.psum(reduced, "dp")
+    value_grad = jnp.sum(lax.all_gather(reduced, "dp"), axis=0)
     return (query_grad, key_grad, value_grad)
 
 

time: 717 us -> 687 us (0.958)
  waiting for transfers between devices: 388 us -> 350 us
    psum x1 -> x0, waiting for transfers between devices: 36.3 us -> none  [per_device(): value_grad = lax.psum(reduced, 'dp')]
  transfers between devices with their start and end apart: 4 -> 3, of which waited for: 4 -> 3; matrix products, arithmetic and copies ran while one was open for 4% -> 4% of each run, Pallas kernels for 0% -> 0%
where the time goes in v1:
time: 687 us; the launch traced here: 679 us
  waiting for transfers between devices  350 us (51%)
  blocking collectives  105 us (15%)
  matrix products  91.9 us (13%)
  local copies, waits for them, and re-layouts  55.6 us (8%)
  other arithmetic  55.5 us (8%)
  between operations  14.6 us (2%)
    reduce_scatter x1, waiting for transfers between devices, per_device(): lax.psum_scatter(partial_value.reshape(lax.axis_size('ctx') * row_share,...  198 us
    all_gather x2, waiting for transfers between devices, entering(): everything = jax.tree.map(lambda part: lax.all_gather(part, axis), value)  152 us
    all_gather x2, blocking collectives, entering(): everything = jax.tree.map(lambda part: lax.all_gather(part, axis), value)  59.5 us
    select_n x64, other arithmetic, turn(): return jax.tree.map(lambda a, b: jnp.where(reached, a, b), new, before)  39.8 us
    unnamed x1, blocking collectives  38.9 us
    dot_general x8, matrix products, second_phase(): lax.dot_general(weights_low, scaled_low, dims_of(0, 0), preferred_element...  14 us
  transfers between devices with their start and end apart: 3, of which 3 were waited for; matrix products, arithmetic and copies ran while one was open for 4% of the time, Pallas kernels for 0%

profile of v1, /device:TPU:1, one launch (start us, length us, event | category | flops | bytes accessed | tf_op | source)
XLA Modules:
  0.0 678.6 jit_solution(14177343074194215215)
XLA Ops:
  7.3 1.2 reduce-window.6
  8.9 1.2 copy.49
  12.6 34.3 %while.72 = (s32[]{:T(128)}, bf16[8,256,256]{1,2,0:T(8,128)(2,1)}, f32[8,256,128]{2,1,0:T(8,128)}, f32[8,256]{1,0:T(8,128)S(1)}, f32[8]{0:T(128)S(1)}, /*index=5...) while((s32[]{:T(128)}, bf16[8,256,256]{1,2,0:T(8,128)(2,1)}, ...), condition=%wide.region_5.6_spmd, body=%wide.region_2.5_spmd.sunk | while | flops 84574080 | bytes 1523417 | solution.py:172
  47.8 2.0 copy.48
  51.3 38.9 %all-reduce = f32[128]{0:T(128)S(1)} all-reduce(f32[128]{0:T(128)S(1)} %dynamic-update-slice), channel_id=2, replica_groups=mesh['dp'=2,'ctx'=16,'tensor'=8] {'ctx'}, use_global_device_ids=true, to_apply=%add | all-reduce | flops 128 | bytes 1024
  90.2 29.2 %all-gather.2 = f32[128,128]{1,0:T(8,128)S(1)} all-gather(f32[8,128]{1,0:T(8,128)S(1)} %get-tuple-element.456), channel_id=4, replica_groups=mesh['dp'=2,'ctx'=16,'tensor'=8] {'ctx'}, dimensions={0}, use_global_device_ids=true | all-gather | bytes 69632 | tf_op jit(solution)/shard_map/all_gather | solution.py:15
  119.4 67.1 %all-gather.9.cloned.1.call-done = f32[128,128,128]{2,1,0:T(8,128)} async-done(((f32[8,128,128]{2,1,0:T(8,128)}), f32[128,128,128]{2,1,0:T(8,128)}) %all-gather.9.cloned.1.call-update) | async-done | bytes 8388624 | tf_op jit(solution)/shard_map/all_gather | solution.py:15
  186.5 20.1 %while.74 = (s32[]{:T(128)}, f32[8,128,128]{2,1,0:T(8,128)S(1)}, f32[8,128]{1,0:T(8,128)S(1)}, s32[]{:T(128)}, f32[16,8]{1,0:T(8,128)S(1)}, /*index=5*/f32[16,8,...) while((s32[]{:T(128)}, f32[8,128,128]{2,1,0:T(8,128)S(1)}, ...), condition=%wide.region_7.8_spmd.clone, body=%wide.region_6.7_spmd.clone.sunk | while | flops 528388 | bytes 1585415 | solution.py:28
  187.7 1.2 fusion.185
  189.0 1.2 fusion.185
  190.3 1.2 fusion.185
  191.5 1.2 fusion.185
  192.8 1.2 fusion.185
  194.0 1.2 fusion.185
  195.3 1.2 fusion.185
  196.5 1.2 fusion.185
  197.8 1.2 fusion.185
  201.6 1.2 fusion.185
  202.8 1.2 fusion.185
  204.1 1.2 fusion.185
  206.6 75.0 %while.73 = (s32[]{:T(128)}, f32[8,256,128]{1,2,0:T(8,128)}, f32[8,256,128]{1,2,0:T(8,128)}, f32[8,256,128]{1,2,0:T(8,128)}, f32[8,128,128]{2,1,0:T(8,128)S(1)},...) while((s32[]{:T(128)}, f32[8,256,128]{1,2,0:T(8,128)}, ...), condition=%wide.region_10.11_spmd, body=%wide.region_8.10_spmd.sunk | while | flops 220071168 | bytes 2862273 | solution.py:183
  212.9 1.7 fusion.181
  222.2 1.8 fusion.181
  231.6 1.8 fusion.181
  241.0 1.8 fusion.181
  250.4 1.8 fusion.181
  259.8 1.8 fusion.181
  269.1 1.7 fusion.181
  278.5 1.8 fusion.181
  282.9 1.7 shift_right_arithmetic.72
  284.6 3.7 fusion.81
  288.3 10.9 %gather_fusion = bf16[256,64,256]{2,1,0:T(8,128)(2,1)} fusion(bf16[128,64,256]{2,1,0:T(8,128)(2,1)} %fusion.81, s32[1024]{0:T(1024)S(1)} %pad_clamp_fusion), kind=kCustom, calls=%fused_computation | custom fusion | bytes 16778240 | tf_op jit(solution)/shard_map/jit(_take)/gather | solution.py:222
  299.5 30.4 %all-gather.4 = f32[128,128]{1,0:T(8,128)S(1)} all-gather(f32[8,128]{1,0:T(8,128)S(1)} %get-tuple-element.464), channel_id=6, replica_groups=mesh['dp'=2,'ctx'=16,'tensor'=8] {'ctx'}, dimensions={0}, use_global_device_ids=true | all-gather | bytes 69632 | tf_op jit(solution)/shard_map/all_gather | solution.py:15
  329.9 84.6 %all-gather.11.cloned.1.call-done = f32[128,128,128]{2,1,0:T(8,128)} async-done(((f32[8,128,128]{2,1,0:T(8,128)}), f32[128,128,128]{2,1,0:T(8,128)}) %all-gather.11.cloned.1.call-update) | async-done | bytes 8388624 | tf_op jit(solution)/shard_map/all_gather | solution.py:15
  414.5 20.1 %while.75 = (s32[]{:T(128)}, f32[8,128,128]{2,1,0:T(8,128)S(1)}, f32[8,128]{1,0:T(8,128)S(1)}, s32[]{:T(128)}, f32[16,8,128,128]{3,2,1,0:T(8,128)}, /*index=5*/f...) while((s32[]{:T(128)}, f32[8,128,128]{2,1,0:T(8,128)S(1)}, ...), condition=%wide.region_12.13_spmd.clone, body=%wide.region_11.12_spmd.clone.sunk | while | flops 528392 | bytes 1585477 | solution.py:28
  418.2 1.2 fusion.188
  419.5 1.2 fusion.188
  425.8 1.2 fusion.188
  427.0 1.2 fusion.188
  433.3 1.2 fusion.188
  435.2 8.6 %fusion.84 = f32[16,16,64,64]{2,3,0,1:T(8,128)} fusion(bf16[256,16,64,1]{0,2,3,1:T(8,128)(2,1)S(1)} %bitcast.308, bf16[16,16,64,256]{3,2,1,0:T(8,128)(2,1)} %bitcast.299, pred[16,16]{1,0:T(8,128)(4,1)S(1)} %copy.63), kind=kOutput, calls=%fused_computation.118 | convolution fusion | flops 541065216 | bytes 13107456 | tf_op jit(solution)/shard_map/snat,tnb->snab/dot_general | solution.py:223
  443.8 9.3 %copy.66 = f32[16,16,64,64]{3,2,1,0:T(8,128)} copy(f32[16,16,64,64]{2,3,0,1:T(8,128)} %fusion.84) | data formatting | bytes 8388608 | tf_op jit(solution)/shard_map/snat,tnb->snab/transpose | solution.py:223
  453.1 8.0 %reshape.164 = f32[16,16,4096]{2,1,0:T(8,128)} reshape(f32[16,16,64,64]{3,2,1,0:T(8,128)} %copy.66) | data formatting | bytes 8388608 | tf_op jit(solution)/shard_map/reshape | solution.py:227
  461.1 1.3 copy.72
  462.4 1.8 fusion.90
  464.6 2.7 multiply_convert_fusion
  467.3 198.0 %reduce-scatter.2.cloned.1.call-done = f32[1,16,4096]{2,1,0:T(8,128)} async-done(((f32[16,16,4096]{2,1,0:T(8,128)}), f32[1,16,4096]{2,1,0:T(8,128)}) %reduce-scatter.2.cloned.1.call-update) | async-done | bytes 262160 | tf_op jit(solution)/shard_map/reduce_scatter | solution.py:226
  665.3 6.1 all-gather.5
  (341 shorter events, 116.7 us)
Async XLA Ops:
  7.2 179.3 %all-gather.9.cloned.1.call-start = ((), (), s32[]{:S(2)}) async-start(), calls=%async_computation.2 | async-start | bytes 8912896 | tf_op jit(solution)/shard_map/all_gather | solution.py:15
  10.1 39.8 %copy-start.6 = (u32[256]{0:T(256)S(1)}, u32[256]{0:T(256)}, u32[]{:S(2)}) copy-start(u32[256]{0:T(256)} %constant.158) | copy-start | bytes 3076
  46.9 0.8 copy-start
  47.7 366.7 %all-gather.11.cloned.1.call-start = ((), (), s32[]{:S(2)}) async-start(), calls=%async_computation.3 | async-start | bytes 8912896 | tf_op jit(solution)/shard_map/all_gather | solution.py:15
  206.6 76.0 %copy-start.5 = (s32[16,16]{1,0:T(8,128)S(1)}, s32[16,16]{1,0:T(8,128)}, u32[]{:S(2)}) copy-start(s32[16,16]{1,0:T(8,128)} %param.25) | copy-start | bytes 3076
  281.6 0.8 copy-start.1
  282.4 382.9 %reduce-scatter.2.cloned.1.call-start = ((), (), s32[]{:S(2)}) async-start(), calls=%async_computation.1 | async-start | bytes 4456448 | tf_op jit(solution)/shard_map/reduce_scatter | solution.py:226
  288.3 146.2 %copy-start.3 = (f32[8,256,128]{1,2,0:T(8,128)S(1)}, f32[8,256,128]{1,2,0:T(8,128)}, u32[]{:S(2)}) copy-start(f32[8,256,128]{1,2,0:T(8,128)} %get-tuple-element.467) | copy-start | bytes 3145732
  453.1 8.0 %copy-start.2 = (f32[8,256,128]{1,2,0:T(8,128)S(1)}, f32[8,256,128]{1,2,0:T(8,128)}, u32[]{:S(2)}) copy-start(f32[8,256,128]{1,2,0:T(8,128)} %get-tuple-element.461) | copy-start | bytes 3145732
  461.1 3.6 copy-start.4
Sparse Core Ops, SparseCore 0:
  47.9 138.5 all-gather.8
  282.5 131.8 all-gather.10
  461.2 204.0 reduce-scatter.1
